TPU v7x, 256 devices: a whole 4x4x8 slice. The times are simulated.
256 devices in a mesh: chain: 8 (over y, core), cols: 32 (over x, z).
Axes of the slice: x: 4, y: 4, z: 8, core: 2. Of those that a mesh axis runs over, the one named last changes fastest.
Arguments:
- factor: float32 [4608, 4608], P(('chain', 'cols')), may hold values from -2 to 2, as said below
- right_side: float32 [4608, 16384], P('chain', 'cols'), may hold values from -6 to 6
- occ_order: int32 [64], replicated, may hold values from 0 to 63, each once
- cabs_order: int32 [256], replicated, may hold values from 0 to 255, each once
Outputs:
- fitted: float32 [64, 256, 4608], P('cols', None, 'chain')
Inputs may be any that keep to these rules, and one draw needn't show every extreme that they name: factor is lower triangular: zero above the diagonal, its diagonal between 1 and 2.
All inputs are finite; a program needn't handle non-finite values.
Results may differ from a plain program's by a relative error of at most 0.00017.
Values sent between devices are 32-bit elements; how exact they have to be, the bound alone decides.
No kernel may reach another device: no remote copies, remote signals or barrier semaphores. Data moves between devices by JAX's collectives and lax.ppermute only.
A program may use at most 128 MiB of HBM per device.

v0:
```python
import jax
import jax.numpy as jnp
from jax import lax
from jax.sharding import PartitionSpec as P


def from_root(value, axis, root):
    return lax.dynamic_index_in_dim(lax.all_gather(value, axis), root, 0, keepdims=False)


def product(left, right):
    return jnp.dot(left, right, precision=lax.Precision.HIGHEST, preferred_element_type=jnp.float32)


def per_device(factor, right_side, occ_order, cabs_order):
    chain_size = lax.axis_size("chain")
    position = lax.axis_index("chain")
    factor_row = lax.all_gather(factor, "cols", axis=0, tiled=True)
    aux_rows = factor_row.shape[0]
    diag_block = lax.dynamic_slice_in_dim(factor_row, position * aux_rows, aux_rows, 1)
    identity = jnp.eye(aux_rows, dtype=jnp.float32)
    inverse = jax.scipy.linalg.solve_triangular(diag_block, identity, lower=True)

    def settle(residual):
        return product(inverse, residual)

    def blank(residual):
        return jnp.zeros_like(residual)

    residual = right_side
    solution = jnp.zeros_like(right_side)
    for section in range(chain_size):
        solved = lax.cond(position == section, settle, blank, residual)
        solution = solution + solved
        if section + 1 < chain_size:
            arrived = from_root(solved, "chain", section)
            coupling = factor_row[:, section * aux_rows : (section + 1) * aux_rows]

            def lower_block(current, arrived=arrived, coupling=coupling):
                return current - product(coupling, arrived)

            def keep_block(current):
                return current

            residual = lax.cond(position > section, lower_block, keep_block, residual)
    occ_total = occ_order.shape[0]
    cabs_local = right_side.shape[1] // occ_total
    cols_size = lax.axis_size("cols")
    occ_local = occ_total // cols_size
    grid = solution.reshape(aux_rows, cabs_local, occ_total)
    grid = jnp.take(grid, occ_order, axis=2)
    grid = grid.reshape(aux_rows, cabs_local, cols_size, occ_local)
    grid = jnp.transpose(grid, (2, 3, 1, 0))
    moved = jnp.take(
        lax.all_to_all(grid, "cols", split_axis=0, concat_axis=2, tiled=True), cabs_order, axis=2
    )
    return moved.reshape(occ_local, moved.shape[2], aux_rows)


def solution(mesh):
    in_specs = (P(("chain", "cols"), None), P("chain", "cols"), P(), P())
    out_specs = P("cols", None, "chain")
    return jax.shard_map(
        per_device, mesh=mesh, in_specs=in_specs, out_specs=out_specs, check_vma=False
    )
```

profile of v0, /device:TPU:33, one launch (start us, length us, event | category | flops | bytes accessed | tf_op | source)
XLA Modules:
  0.0 740.3 jit_solution(2091140109980776723)
XLA Ops:
  6.5 1.3 copy.126
  9.3 128.3 %all-gather.31.cloned.1.call-done = f32[32,18,4608]{2,1,0:T(8,128)} async-done(((f32[1,18,4608]{2,1,0:T(8,128)}), f32[32,18,4608]{2,1,0:T(8,128)}) %all-gather.31.cloned.1.call-update) | async-done | bytes 10616848 | tf_op jit(solution)/shard_map/all_gather | solution.py:18
  137.6 11.4 %reshape.89 = f32[576,4608]{1,0:T(8,128)} reshape(f32[32,18,4608]{2,1,0:T(8,128)} %all-gather.31.cloned.1.call-done) | data formatting | bytes 21233664
  149.0 1.8 dynamic-slice_select_fusion
  150.7 10.5 %while.1 = (s32[]{:T(128)}, f32[576,576]{1,0:T(8,128)S(1)}, s32[4,2]{0,1:T(2,128)S(1)}, f32[4,128,128]{2,1,0:T(8,128)}, s32[]{:T(128)}) while((s32[]{:T(128)}, f32[576,576]{1,0:T(8,128)S(1)}, s32[4,2]{0,1:T(2,128)S(1)}, f32[4,128,128]{2,1,0:T(8,128)}, s32[]{:T(128)}) %tuple.169), condition=%wide.while_cond, body=%wide.while_body.sunk | while | flops 2 | bytes 132705 | solution.py:22
  151.4 2.0 bitcast_dynamic-update-slice_fusion.2
  154.0 2.0 bitcast_dynamic-update-slice_fusion.2
  156.7 2.0 bitcast_dynamic-update-slice_fusion.2
  159.3 2.0 bitcast_dynamic-update-slice_fusion.2
  162.6 49.8 %custom-call.4 = f32[5,128,128]{1,2,0:T(8,128)} custom-call(f32[5,128,128]{2,1,0:T(8,128)S(1)} %pad_maximum_fusion), custom_call_target="InvertDiagBlocksLowerTriangular" | custom-call | tf_op jit(solution)/shard_map/jit(_solve_triangular)/triangular_solve | solution.py:22
  213.6 1.4 convolution_subtract_fusion.1
  215.0 1.3 constant_dynamic-update-slice_fusion.2
  216.3 1.5 convolution_subtract_fusion
  218.2 1.9 convolution_subtract_fusion.2
  220.5 2.0 fusion.57
  224.1 56.9 %all-gather.17.cloned.1.call-done = f32[4608,512]{1,0:T(8,128)} async-done(((f32[576,512]{1,0:T(8,128)}), f32[4608,512]{1,0:T(8,128)}) %all-gather.17.cloned.1.call-update) | async-done | bytes 9437200 | tf_op jit(solution)/shard_map/all_gather | solution.py:8
  281.0 5.0 conditional.16
  281.2 4.8 fusion.2
  286.0 4.1 conditional.17
  286.0 4.1 fusion.84
  290.2 55.5 %all-gather.19.cloned.1.call-done = f32[4608,512]{1,0:T(8,128)} async-done(((f32[576,512]{1,0:T(8,128)}), f32[4608,512]{1,0:T(8,128)}) %all-gather.19.cloned.1.call-update) | async-done | bytes 9437200 | tf_op jit(solution)/shard_map/all_gather | solution.py:8
  347.0 63.7 %all-gather.21.cloned.1.call-done = f32[4608,512]{1,0:T(8,128)} async-done(((f32[576,512]{1,0:T(8,128)}), f32[4608,512]{1,0:T(8,128)}) %all-gather.21.cloned.1.call-update) | async-done | bytes 9437200 | tf_op jit(solution)/shard_map/all_gather | solution.py:8
  412.4 63.4 %all-gather.23.cloned.1.call-done = f32[4608,512]{1,0:T(8,128)} async-done(((f32[576,512]{1,0:T(8,128)}), f32[4608,512]{1,0:T(8,128)}) %all-gather.23.cloned.1.call-update) | async-done | bytes 9437200 | tf_op jit(solution)/shard_map/all_gather | solution.py:8
  477.1 64.9 %all-gather.25.cloned.1.call-done = f32[4608,512]{1,0:T(8,128)} async-done(((f32[576,512]{1,0:T(8,128)}), f32[4608,512]{1,0:T(8,128)}) %all-gather.25.cloned.1.call-update) | async-done | bytes 9437200 | tf_op jit(solution)/shard_map/all_gather | solution.py:8
  543.4 64.6 %all-gather.27.cloned.1.call-done = f32[4608,512]{1,0:T(8,128)} async-done(((f32[576,512]{1,0:T(8,128)}), f32[4608,512]{1,0:T(8,128)}) %all-gather.27.cloned.1.call-update) | async-done | bytes 9437200 | tf_op jit(solution)/shard_map/all_gather | solution.py:8
  609.4 63.8 %all-gather.29.cloned.1.call-done = f32[4608,512]{1,0:T(8,128)} async-done(((f32[576,512]{1,0:T(8,128)}), f32[4608,512]{1,0:T(8,128)}) %all-gather.29.cloned.1.call-update) | async-done | bytes 9437200 | tf_op jit(solution)/shard_map/all_gather | solution.py:8
  674.6 4.9 add_add_fusion
  681.3 1.2 select_bitcast_fusion.1
  682.6 9.9 %all-to-all-start = ((f32[32,2,8,576]{3,2,1,0:T(8,128)}), f32[32,2,8,576]{3,2,1,0:T(8,128)S(1)}, u32[]{:S(2)}, u32[]{:S(2)}) async-start(f32[32,2,8,576]{3,2,1,0:T(8,128)} %select_bitcast_fusion.1), calls=%async_computation | async-start | bytes 2621440 | tf_op jit(solution)/shard_map/all_to_all | solution.py:55
  692.5 34.0 %all-to-all-done = f32[32,2,8,576]{3,2,1,0:T(8,128)S(1)} async-done(((f32[32,2,8,576]{3,2,1,0:T(8,128)}), f32[32,2,8,576]{3,2,1,0:T(8,128)S(1)}, u32[]{:S(2)}, u32[]{:S(2)}) %all-to-all-start) | async-done | bytes 1179680 | tf_op jit(solution)/shard_map/all_to_all | solution.py:55
  727.5 2.2 gather_fusion.1
  730.8 2.2 copy.71
  (80 shorter events, 29.6 us)
Async XLA Ops:
  6.5 131.1 %all-gather.31.cloned.1.call-start = ((), (), s32[]{:S(2)}) async-start(), calls=%async_computation.8 | async-start | bytes 14598144 | tf_op jit(solution)/shard_map/all_gather | solution.py:18
  7.8 273.2 %all-gather.17.cloned.1.call-start = ((), (), s32[]{:S(2)}) async-start(), calls=%async_computation.1 | async-start | bytes 10616832 | tf_op jit(solution)/shard_map/all_gather | solution.py:8
  161.3 1.3 copy-start.1
  212.3 4.0 copy-start
  215.0 2.9 copy-start.2
  224.1 121.7 %all-gather.19.cloned.1.call-start = ((), (), s32[]{:S(2)}) async-start(), calls=%async_computation.2 | async-start | bytes 10616832 | tf_op jit(solution)/shard_map/all_gather | solution.py:8
  290.1 120.5 %all-gather.21.cloned.1.call-start = ((), (), s32[]{:S(2)}) async-start(), calls=%async_computation.3 | async-start | bytes 10616832 | tf_op jit(solution)/shard_map/all_gather | solution.py:8
  347.0 128.8 %all-gather.23.cloned.1.call-start = ((), (), s32[]{:S(2)}) async-start(), calls=%async_computation.4 | async-start | bytes 10616832 | tf_op jit(solution)/shard_map/all_gather | solution.py:8
  412.4 129.6 %all-gather.25.cloned.1.call-start = ((), (), s32[]{:S(2)}) async-start(), calls=%async_computation.5 | async-start | bytes 10616832 | tf_op jit(solution)/shard_map/all_gather | solution.py:8
  477.0 131.0 %all-gather.27.cloned.1.call-start = ((), (), s32[]{:S(2)}) async-start(), calls=%async_computation.6 | async-start | bytes 10616832 | tf_op jit(solution)/shard_map/all_gather | solution.py:8
  543.3 129.9 %all-gather.29.cloned.1.call-start = ((), (), s32[]{:S(2)}) async-start(), calls=%async_computation.7 | async-start | bytes 10616832 | tf_op jit(solution)/shard_map/all_gather | solution.py:8
  608.0 1.2 copy-start.4
  608.0 1.3 copy-start.3
  682.6 43.8 %all-to-all-start = ((f32[32,2,8,576]{3,2,1,0:T(8,128)}), f32[32,2,8,576]{3,2,1,0:T(8,128)S(1)}, u32[]{:S(2)}, u32[]{:S(2)}) async-start(f32[32,2,8,576]{3,2,1,0:T(8,128)} %select_bitcast_fusion.1), calls=%async_computation | async-start | bytes 2621440 | tf_op jit(solution)/shard_map/all_to_all | solution.py:55
Sparse Core Ops, SparseCore 0:
  9.9 127.6 all-gather.30
  224.2 56.7 all-gather.16
  290.3 55.4 all-gather.18
  347.4 63.2 all-gather.20
  412.5 63.2 all-gather.22
  477.5 64.4 all-gather.24
  543.8 64.1 all-gather.26
  609.9 63.3 all-gather.28
where the time goes:
time: 749 us; the launch traced here: 740 us
  waiting for transfers between devices  595 us (79%)
  other arithmetic  61.4 us (8%)
  local copies, waits for them, and re-layouts  38.8 us (5%)
  matrix products  19.3 us (3%)
  between operations  14.3 us (2%)
  starting transfers between devices  10.1 us (1%)
    all_gather x7, waiting for transfers between devices, from_root(): lax.all_gather(value, axis)  433 us
    all_gather x1, waiting for transfers between devices, per_device(): factor_row = lax.all_gather(factor, 'cols', axis=0, tiled=True)  128 us
    another operation x7, other arithmetic, per_device(): jax.scipy.linalg.solve_triangular(diag_block, identity, lower=True)  52.8 us
    all_to_all x1, waiting for transfers between devices, per_device(): lax.all_to_all(grid, 'cols', split_axis=0, concat_axis=2, tiled=True)  34 us
    another operation x19, local copies, waits for them, and re-layouts  18.8 us
  transfers between devices with their start and end apart: 9, of which 9 were waited for; matrix products, arithmetic and copies ran while one was open for 0% of the time, Pallas kernels for 0%

commit v1 on v0

--- a/solution.py
+++ b/solution.py
@@ -15,7 +15,9 @@
 def per_device(factor, right_side, occ_order, cabs_order):
     chain_size = lax.axis_size("chain")
     position = lax.axis_index("chain")
-    factor_row = lax.all_gather(factor, "cols", axis=0, tiled=True)
+    factor_row = jnp.concatenate(
+        lax.all_to_all(jnp.stack([factor] * lax.axis_size("cols"), axis=0), "cols", 0, 0), axis=0
+    )
     aux_rows = factor_row.shape[0]
     diag_block = lax.dynamic_slice_in_dim(factor_row, position * aux_rows, aux_rows, 1)
     identity = jnp.eye(aux_rows, dtype=jnp.float32)

time: 749 us -> 971 us (1.30)
  waiting for transfers between devices: 595 us -> 801 us
  starting transfers between devices: 10.1 us -> 20.8 us
    all_to_all x0 -> x1, waiting for transfers between devices: none -> 315 us  [per_device(): lax.all_to_all(jnp.stack([factor] * lax.axis_size('cols'), axis=0), 'cols...]
    all_gather x1 -> x0, waiting for transfers between devices: 128 us -> none  [per_device(): factor_row = lax.all_gather(factor, 'cols', axis=0, tiled=True)]
    all_gather x7, waiting for transfers between devices: 433 us -> 452 us  [from_root(): lax.all_gather(value, axis)]
    reshape x0 -> x1, local copies, waits for them, and re-layouts: none -> 11.4 us  [per_device(): jnp.concatenate(lax.all_to_all(jnp.stack([factor] * lax.axis_size('cols')...]
    unnamed x12 -> x13, local copies, waits for them, and re-layouts: 12.7 us -> 1.39 us
    all_to_all x0 -> x1, starting transfers between devices: none -> 10.7 us  [per_device(): lax.all_to_all(jnp.stack([factor] * lax.axis_size('cols'), axis=0), 'cols...]
    another operation x19 -> x20, local copies, waits for them, and re-layouts: 18.8 us -> 25.8 us
where the time goes in v1:
time: 971 us; the launch traced here: 964 us
  waiting for transfers between devices  801 us (82%)
  other arithmetic  61.5 us (6%)
  local copies, waits for them, and re-layouts  45.9 us (5%)
  starting transfers between devices  20.8 us (2%)
  matrix products  19.3 us (2%)
  between operations  14.3 us (1%)
    all_gather x7, waiting for transfers between devices, from_root(): lax.all_gather(value, axis)  452 us
    all_to_all x1, waiting for transfers between devices, per_device(): lax.all_to_all(jnp.stack([factor] * lax.axis_size('cols'), axis=0), 'cols...  315 us
    another operation x7, other arithmetic, per_device(): jax.scipy.linalg.solve_triangular(diag_block, identity, lower=True)  52.8 us
    all_to_all x1, waiting for transfers between devices, per_device(): lax.all_to_all(grid, 'cols', split_axis=0, concat_axis=2, tiled=True)  34 us
  transfers between devices with their start and end apart: 9, of which 9 were waited for; matrix products, arithmetic and copies ran while one was open for 0% of the time, Pallas kernels for 0%

profile of v1, /device:TPU:33, one launch (start us, length us, event | category | flops | bytes accessed | tf_op | source)
XLA Modules:
  0.0 963.5 jit_solution(696763191808955021)
XLA Ops:
  7.9 6.8 stack.2
  14.7 10.7 %all-to-all-start = ((f32[32,18,4608]{2,1,0:T(8,128)}), f32[32,18,4608]{2,1,0:T(8,128)}, u32[]{:S(2)}, u32[]{:S(2)}) async-start(f32[32,18,4608]{2,1,0:T(8,128)} %stack.2), calls=%async_computation | async-start | bytes 28311552 | tf_op jit(solution)/shard_map/all_to_all | solution.py:19
  26.8 314.5 %all-to-all-done = f32[32,18,4608]{2,1,0:T(8,128)} async-done(((f32[32,18,4608]{2,1,0:T(8,128)}), f32[32,18,4608]{2,1,0:T(8,128)}, u32[]{:S(2)}, u32[]{:S(2)}) %all-to-all-start) | async-done | bytes 10616864 | tf_op jit(solution)/shard_map/all_to_all | solution.py:19
  341.4 11.4 %reshape.44 = f32[576,4608]{1,0:T(8,128)} reshape(f32[32,18,4608]{2,1,0:T(8,128)} %all-to-all-done) | data formatting | bytes 21233664 | tf_op jit(solution)/shard_map/reshape | solution.py:18
  352.7 1.8 dynamic-slice_select_fusion
  354.5 10.8 %while.1 = (s32[]{:T(128)}, f32[576,576]{1,0:T(8,128)S(1)}, s32[4,2]{0,1:T(2,128)S(1)}, f32[4,128,128]{2,1,0:T(8,128)}, s32[]{:T(128)}) while((s32[]{:T(128)}, f32[576,576]{1,0:T(8,128)S(1)}, s32[4,2]{0,1:T(2,128)S(1)}, f32[4,128,128]{2,1,0:T(8,128)}, s32[]{:T(128)}) %tuple.161), condition=%wide.while_cond, body=%wide.while_body.sunk | while | flops 2 | bytes 132705 | solution.py:24
  355.2 2.0 bitcast_dynamic-update-slice_fusion.2
  357.9 2.0 bitcast_dynamic-update-slice_fusion.2
  360.5 2.0 bitcast_dynamic-update-slice_fusion.2
  363.2 2.0 bitcast_dynamic-update-slice_fusion.2
  366.5 49.8 %custom-call.4 = f32[5,128,128]{1,2,0:T(8,128)} custom-call(f32[5,128,128]{2,1,0:T(8,128)S(1)} %pad_maximum_fusion), custom_call_target="InvertDiagBlocksLowerTriangular" | custom-call | tf_op jit(solution)/shard_map/jit(_solve_triangular)/triangular_solve | solution.py:24
  417.5 1.4 convolution_subtract_fusion.1
  420.3 1.5 convolution_subtract_fusion
  422.2 1.9 convolution_subtract_fusion.2
  424.5 2.0 fusion.57
  428.3 76.1 %all-gather.15.cloned.1.call-done = f32[4608,512]{1,0:T(8,128)} async-done(((f32[576,512]{1,0:T(8,128)}), f32[4608,512]{1,0:T(8,128)}) %all-gather.15.cloned.1.call-update) | async-done | bytes 9437200 | tf_op jit(solution)/shard_map/all_gather | solution.py:8
  504.4 4.8 conditional.16
  504.4 4.8 fusion.2
  509.2 4.1 conditional.17
  509.2 4.1 fusion.84
  513.4 55.5 %all-gather.17.cloned.1.call-done = f32[4608,512]{1,0:T(8,128)} async-done(((f32[576,512]{1,0:T(8,128)}), f32[4608,512]{1,0:T(8,128)}) %all-gather.17.cloned.1.call-update) | async-done | bytes 9437200 | tf_op jit(solution)/shard_map/all_gather | solution.py:8
  568.9 1.6 conditional.19
  570.6 63.7 %all-gather.19.cloned.1.call-done = f32[4608,512]{1,0:T(8,128)} async-done(((f32[576,512]{1,0:T(8,128)}), f32[4608,512]{1,0:T(8,128)}) %all-gather.19.cloned.1.call-update) | async-done | bytes 9437200 | tf_op jit(solution)/shard_map/all_gather | solution.py:8
  635.6 63.4 %all-gather.21.cloned.1.call-done = f32[4608,512]{1,0:T(8,128)} async-done(((f32[576,512]{1,0:T(8,128)}), f32[4608,512]{1,0:T(8,128)}) %all-gather.21.cloned.1.call-update) | async-done | bytes 9437200 | tf_op jit(solution)/shard_map/all_gather | solution.py:8
  700.4 64.9 %all-gather.23.cloned.1.call-done = f32[4608,512]{1,0:T(8,128)} async-done(((f32[576,512]{1,0:T(8,128)}), f32[4608,512]{1,0:T(8,128)}) %all-gather.23.cloned.1.call-update) | async-done | bytes 9437200 | tf_op jit(solution)/shard_map/all_gather | solution.py:8
  766.6 64.7 %all-gather.25.cloned.1.call-done = f32[4608,512]{1,0:T(8,128)} async-done(((f32[576,512]{1,0:T(8,128)}), f32[4608,512]{1,0:T(8,128)}) %all-gather.25.cloned.1.call-update) | async-done | bytes 9437200 | tf_op jit(solution)/shard_map/all_gather | solution.py:8
  832.8 63.8 %all-gather.27.cloned.1.call-done = f32[4608,512]{1,0:T(8,128)} async-done(((f32[576,512]{1,0:T(8,128)}), f32[4608,512]{1,0:T(8,128)}) %all-gather.27.cloned.1.call-update) | async-done | bytes 9437200 | tf_op jit(solution)/shard_map/all_gather | solution.py:8
  897.9 4.9 add_add_fusion
  905.8 9.9 %all-to-all-start.1 = ((f32[32,2,8,576]{3,2,1,0:T(8,128)}), f32[32,2,8,576]{3,2,1,0:T(8,128)S(1)}, u32[]{:S(2)}, u32[]{:S(2)}) async-start(f32[32,2,8,576]{3,2,1,0:T(8,128)} %select_bitcast_fusion.1), calls=%async_computation.1 | async-start | bytes 2621440 | tf_op jit(solution)/shard_map/all_to_all | solution.py:57
  915.7 34.0 %all-to-all-done.1 = f32[32,2,8,576]{3,2,1,0:T(8,128)S(1)} async-done(((f32[32,2,8,576]{3,2,1,0:T(8,128)}), f32[32,2,8,576]{3,2,1,0:T(8,128)S(1)}, u32[]{:S(2)}, u32[]{:S(2)}) %all-to-all-start.1) | async-done | bytes 1179680 | tf_op jit(solution)/shard_map/all_to_all | solution.py:57
  950.8 2.2 gather_fusion.1
  954.1 2.2 copy.49
  (82 shorter events, 32.1 us)
Async XLA Ops:
  6.5 1.4 copy-start.2
  14.7 326.7 %all-to-all-start = ((f32[32,18,4608]{2,1,0:T(8,128)}), f32[32,18,4608]{2,1,0:T(8,128)}, u32[]{:S(2)}, u32[]{:S(2)}) async-start(f32[32,18,4608]{2,1,0:T(8,128)} %stack.2), calls=%async_computation | async-start | bytes 28311552 | tf_op jit(solution)/shard_map/all_to_all | solution.py:19
  25.4 479.1 %all-gather.15.cloned.1.call-start = ((), (), s32[]{:S(2)}) async-start(), calls=%async_computation.2 | async-start | bytes 10616832 | tf_op jit(solution)/shard_map/all_gather | solution.py:8
  365.2 1.3 copy-start.1
  416.3 4.0 copy-start
  418.9 2.9 copy-start.3
  428.2 140.7 %all-gather.17.cloned.1.call-start = ((), (), s32[]{:S(2)}) async-start(), calls=%async_computation.3 | async-start | bytes 10616832 | tf_op jit(solution)/shard_map/all_gather | solution.py:8
  513.3 121.0 %all-gather.19.cloned.1.call-start = ((), (), s32[]{:S(2)}) async-start(), calls=%async_computation.4 | async-start | bytes 10616832 | tf_op jit(solution)/shard_map/all_gather | solution.py:8
  570.6 128.5 %all-gather.21.cloned.1.call-start = ((), (), s32[]{:S(2)}) async-start(), calls=%async_computation.5 | async-start | bytes 10616832 | tf_op jit(solution)/shard_map/all_gather | solution.py:8
  635.5 129.8 %all-gather.23.cloned.1.call-start = ((), (), s32[]{:S(2)}) async-start(), calls=%async_computation.6 | async-start | bytes 10616832 | tf_op jit(solution)/shard_map/all_gather | solution.py:8
  700.4 130.9 %all-gather.25.cloned.1.call-start = ((), (), s32[]{:S(2)}) async-start(), calls=%async_computation.7 | async-start | bytes 10616832 | tf_op jit(solution)/shard_map/all_gather | solution.py:8
  766.6 130.1 %all-gather.27.cloned.1.call-start = ((), (), s32[]{:S(2)}) async-start(), calls=%async_computation.8 | async-start | bytes 10616832 | tf_op jit(solution)/shard_map/all_gather | solution.py:8
  831.3 1.4 copy-start.5
  831.3 1.5 copy-start.4
  905.8 43.8 %all-to-all-start.1 = ((f32[32,2,8,576]{3,2,1,0:T(8,128)}), f32[32,2,8,576]{3,2,1,0:T(8,128)S(1)}, u32[]{:S(2)}, u32[]{:S(2)}) async-start(f32[32,2,8,576]{3,2,1,0:T(8,128)} %select_bitcast_fusion.1), calls=%async_computation.1 | async-start | bytes 2621440 | tf_op jit(solution)/shard_map/all_to_all | solution.py:57
Sparse Core Ops, SparseCore 0:
  428.4 76.0 all-gather.14
  513.5 55.4 all-gather.16
  570.8 63.4 all-gather.18
  636.0 63.0 all-gather.20
  700.7 64.5 all-gather.22
  767.0 64.1 all-gather.24
  833.1 63.5 all-gather.26
